TPU v7x, 32 devices: a whole 2x2x4 slice. The times are simulated.
32 devices in a mesh: grp: 2 (over y), feat: 4 (over z), samp: 4 (over x, core).
Axes of the slice: x: 2, y: 2, z: 4, core: 2. Of those that a mesh axis runs over, the one named last changes fastest.
Arguments:
- embeddings: bfloat16 [8192, 1024], P(('grp', 'samp')), parts along dimension 0, may hold values from -6 to 6
- sign_bits: int32 [4096], P('feat'), may hold values 0 or 1
- perms: int32 [4, 1024], P('feat'), may hold values from 0 to 1023, each once within a row
- gauss: float32 [4096], P('feat'), may hold values from -4 to 4
- scale: float32 [4096], P('feat'), may hold values from 0.5 to 2
- phase: float32 [4096], P('feat'), may hold values from -3.140625 to 3.140625
- basis: float32 [128, 4096], P('grp', 'feat'), parts along dimension 0, may hold values from -40 to 40
Outputs:
- basis_out: float32 [128, 4096], P('grp', 'feat'), parts along dimension 0
- projections: float32 [128, 4096], P('grp', 'samp'), parts along dimension 0
There are 2 independent parts, one for each index of `grp`. A program takes and returns all parts, laid end to end along the dimension named above; an argument that names none is the same for every part. Nothing has to cross between parts.
Inputs may be any that keep to these rules, and one draw needn't show every extreme that they name: Each row of perms names every number of 0 to 1023 once.
All inputs are finite; a program needn't handle non-finite values. No bound on the sum of `sign_bits` on one device may be relied on, other than what follows from the above.
Results may differ from a plain program's by a relative error of at most 0.0057.
Values sent between devices are 32-bit elements; how exact they have to be, the bound alone decides.
A program may use at most 64 MiB of HBM per device.

v0:
```python
import math
import jax
import jax.numpy as jnp
from jax import lax
from jax.sharding import PartitionSpec as P


def sylvester(width):
    indices = lax.iota(jnp.int32, width)
    parity = jnp.zeros((width, width), jnp.int32)
    for position in range(width.bit_length() - 1):
        row_bits = jnp.right_shift(indices[:, None], position) & 1
        col_bits = jnp.right_shift(indices[None, :], position) & 1
        parity = parity + row_bits * col_bits
    return jnp.where(parity % 2 == 0, 1.0, -1.0).astype(jnp.bfloat16)


def cholesky_step(grown, total):
    local_gram = jnp.dot(grown, grown.T, precision=lax.Precision.HIGHEST)
    gram = lax.psum(local_gram, "feat")
    lower = jnp.linalg.cholesky(gram / total)
    return jax.scipy.linalg.solve_triangular(lower, grown, lower=True)


def local(embeddings, sign_bits, perms, gauss, scale, phase, basis):
    width = embeddings.shape[1]
    rows = embeddings.shape[0]
    table = sylvester(width)
    features_total = width * lax.axis_size("feat")
    span_total = rows * lax.axis_size("samp")
    signs = (2 * sign_bits - 1).astype(jnp.bfloat16)
    first = jnp.dot(embeddings * signs, table, preferred_element_type=jnp.float32).astype(
        jnp.bfloat16
    )
    reorder = (lax.iota(jnp.int32, width)[:, None] == perms[0][None, :]).astype(jnp.bfloat16)
    picked = jnp.dot(first, reorder, preferred_element_type=jnp.float32)
    mixed = (picked * gauss).astype(jnp.bfloat16)
    freq = jnp.dot(mixed, table, preferred_element_type=jnp.float32) * scale / width + phase
    features = (math.sqrt(2.0) * jnp.cos(freq)).astype(jnp.bfloat16)
    basis_low = basis.astype(jnp.bfloat16)
    partial_scores = lax.dot_general(
        basis_low, features, (((1,), (1,)), ((), ())), preferred_element_type=jnp.float32
    )
    summed = lax.psum(partial_scores, "feat")
    projections = summed / math.sqrt(features_total)
    proj_low = projections.astype(jnp.bfloat16)
    update_part = jnp.dot(proj_low, features, preferred_element_type=jnp.float32)
    update = lax.psum(update_part, "samp")
    grown = basis + update / math.sqrt(span_total)
    basis_out = cholesky_step(grown, features_total)
    return (basis_out, projections)


def solution(mesh):
    placed = (
        P(("grp", "samp"), None),
        P("feat"),
        P("feat", None),
        P("feat"),
        P("feat"),
        P("feat"),
        P("grp", "feat"),
    )
    return jax.shard_map(
        local,
        mesh=mesh,
        in_specs=placed,
        out_specs=(P("grp", "feat"), P("grp", "samp")),
        check_vma=False,
    )
```

profile of v0, /device:TPU:0, one launch (start us, length us, event | category | flops | bytes accessed | tf_op | source)
XLA Modules:
  0.0 159.9 jit_solution(12361996061334306493)
XLA Ops:
  7.2 0.0 all-reduce.3.cloned.1.call-start
  7.3 0.7 add_convert_fusion
  8.0 1.5 iota_compare_fusion.7
  9.5 0.0 copy-start.2
  9.5 0.0 copy-start.3
  9.5 0.0 copy-start.4
  9.5 12.2 %fusion.2 = f32[1024,1024]{1,0:T(8,128)} fusion(bf16[1024,1024]{1,0:T(8,128)(2,1)} %param.7, bf16[1024]{0:T(1024)(128)(2,1)S(1)} %add_convert_fusion, s32[1024]{0:T(1024)S(1)} %get-tuple-element.2, s32[1024]{0:T(1024)S(1)} %get-tuple-element.3, s32[1024]{0:T(1024)S(1)} %get-tuple-element.4, s32[1024]{0:T(1024)S(1)} %get-tuple-element.5, ...), kind=kOutput, calls=%fused_computation.9 | convolution fusion | flops 4331667456 | bytes 7383040 | tf_op jit(solution)/shard_map/dot_general | solution.py:36
  21.7 0.0 copy-done.2
  21.7 0.0 copy-done.3
  21.7 0.0 copy-done.4
  21.7 0.0 copy-start
  21.7 22.2 %multiply_convert_fusion = bf16[1024,1024]{1,0:T(8,128)(2,1)S(1)} fusion(f32[1024,1024]{1,0:T(8,128)} %fusion.2, f32[1024]{0:T(1024)S(1)} %copy-done.2, f32[1024]{0:T(1024)S(1)} %copy-done.3, f32[1024]{0:T(1024)S(1)} %copy-done.4, s32[1024]{0:T(1024)S(1)} %get-tuple-element.2, s32[1024]{0:T(1024)S(1)} %get-tuple-element.3, s32[1024]{0:T(1024)S(1)} %get-tuple-element.4, ...), kind=kOutput, calls=%fused_computation.5 | convolution fusion | flops 2189426688 | bytes 6344704 | tf_op jit(solution)/shard_map/dot_general | solution.py:38
  44.0 0.0 copy-done
  44.0 1.5 convolution_bitcast_fusion
  45.4 0.0 all-reduce.3.cloned.1.call-update
  45.5 0.0 all-reduce.5.cloned.1.call-start
  45.5 38.1 %all-reduce.3.cloned.1.call-done = f32[64,1024]{1,0:T(8,128)} async-done(((f32[64,1024]{1,0:T(8,128)}), f32[64,1024]{1,0:T(8,128)}) %all-reduce.3.cloned.1.call-update) | async-done | bytes 262160 | tf_op jit(solution)/shard_map/psum | solution.py:44
  83.6 1.0 broadcast_multiply_fusion
  84.6 0.0 copy-start.1
  84.6 1.2 fusion.14
  85.8 0.0 all-reduce.5.cloned.1.call-update
  85.8 32.5 %all-reduce.5.cloned.1.call-done = f32[64,1024]{1,0:T(8,128)} async-done(((f32[64,1024]{1,0:T(8,128)}), f32[64,1024]{1,0:T(8,128)}) %all-reduce.5.cloned.1.call-update) | async-done | bytes 262160 | tf_op jit(solution)/shard_map/psum | solution.py:48
  118.4 1.4 fusion.18
  119.8 19.0 %psum.23 = f32[64,64]{0,1:T(8,128)S(1)} all-reduce(f32[64,64]{0,1:T(8,128)S(1)} %fusion.18), channel_id=1, replica_groups=mesh['grp'=2,'feat'=4,'samp'=4] {'feat'}, use_global_device_ids=true, to_apply=%region_2.3 | all-reduce | flops 4096 | bytes 32768 | tf_op jit(solution)/shard_map/psum | solution.py:20
  138.8 0.1 copy.10
  138.9 5.8 %cholesky.16 = f32[64,64]{1,0:T(8,128)S(1)} custom-call(f32[64,64]{1,0:T(8,128)S(1)} %fusion.21), custom_call_target="Cholesky" | custom-call | tf_op jit(solution)/shard_map/jit(cholesky)/cholesky | solution.py:21
  144.7 0.6 compare_reduce_fusion
  145.4 0.7 fusion.19
  146.1 4.9 %custom-call.7 = f32[1,64,64]{1,2,0:T(8,128)S(1)} custom-call(f32[1,64,64]{2,1,0:T(8,128)S(1)} %fusion.19), custom_call_target="InvertDiagBlocksLowerTriangular" | custom-call | tf_op jit(solution)/shard_map/jit(_solve_triangular)/triangular_solve | solution.py:22
  150.9 2.1 %fusion.17 = f32[64,1024]{1,0:T(8,128)} fusion(f32[64,1024]{1,0:T(8,128)S(1)} %copy-done, f32[64,1024]{1,0:T(8,128)} %all-reduce.5.cloned.1.call-done, f32[1,64,64]{1,2,0:T(8,128)S(1)} %custom-call.7), kind=kOutput, calls=%fused_computation.22 | convolution fusion | flops 50462720 | bytes 802816 | tf_op jit(solution)/shard_map/jit(_solve_triangular)/triangular_solve | solution.py:22
  153.0 0.0 copy-done.1
  (8 shorter events, 0.1 us)
Async XLA Ops:
  7.2 76.5 %all-reduce.3.cloned.1.call-start = ((), (), s32[]{:S(2)}) async-start(), calls=%async_computation | async-start | bytes 524288 | tf_op jit(solution)/shard_map/psum | solution.py:44
  9.5 12.3 %copy-start.2 = (f32[1024]{0:T(1024)S(1)}, f32[1024]{0:T(1024)}, u32[]{:S(2)}) copy-start(f32[1024]{0:T(1024)} %param.12) | copy-start | bytes 12292
  9.5 12.3 %copy-start.3 = (f32[1024]{0:T(1024)S(1)}, f32[1024]{0:T(1024)}, u32[]{:S(2)}) copy-start(f32[1024]{0:T(1024)} %param.11) | copy-start | bytes 12292
  9.5 12.3 %copy-start.4 = (f32[1024]{0:T(1024)S(1)}, f32[1024]{0:T(1024)}, u32[]{:S(2)}) copy-start(f32[1024]{0:T(1024)} %param.10) | copy-start | bytes 12292
  21.7 22.2 %copy-start = (f32[64,1024]{1,0:T(8,128)S(1)}, f32[64,1024]{1,0:T(8,128)}, u32[]{:S(2)}) copy-start(f32[64,1024]{1,0:T(8,128)} %param.13) | copy-start | bytes 786436
  45.5 72.9 %all-reduce.5.cloned.1.call-start = ((), (), s32[]{:S(2)}) async-start(), calls=%async_computation.1 | async-start | bytes 524288 | tf_op jit(solution)/shard_map/psum | solution.py:48
  84.6 68.4 %copy-start.1 = (f32[64,1024]{1,0:T(8,128)}, f32[64,1024]{1,0:T(8,128)S(1)}, u32[]{:S(2)}) copy-start(f32[64,1024]{1,0:T(8,128)S(1)} %broadcast_multiply_fusion) | copy-start | bytes 786436
Sparse Core Ops, SparseCore 0:
  45.6 37.9 all-reduce.2
  86.6 31.6 all-reduce.4
where the time goes:
time: 160 us
  waiting for transfers between devices  70.7 us (44%)
  matrix products  40.6 us (25%)
  blocking collectives  19 us (12%)
  other arithmetic  15.3 us (10%)
  between operations  14.2 us (9%)
    psum x1, waiting for transfers between devices, local(): summed = lax.psum(partial_scores, 'feat')  38.1 us
    psum x1, waiting for transfers between devices, local(): update = lax.psum(update_part, 'samp')  32.5 us
    dot_general x1, matrix products, local(): jnp.dot(mixed, table, preferred_element_type=jnp.float32) * scale / width  22.2 us
    psum x1, blocking collectives, cholesky_step(): gram = lax.psum(local_gram, 'feat')  19 us
    dot_general x1, matrix products, local(): picked = jnp.dot(first, reorder, preferred_element_type=jnp.float32)  12.2 us
    another operation x3, other arithmetic, cholesky_step(): lower = jnp.linalg.cholesky(gram / total)  6.52 us
    another operation x2, other arithmetic, cholesky_step(): return jax.scipy.linalg.solve_triangular(lower, grown, lower=True)  5.55 us
  transfers between devices with their start and end apart: 2, of which 2 were waited for; matrix products, arithmetic and copies ran while one was open for 0% of the time, Pallas kernels for 0%

commit v1 on v0

--- a/solution.py
+++ b/solution.py
@@ -45,7 +45,7 @@
     projections = summed / math.sqrt(features_total)
     proj_low = projections.astype(jnp.bfloat16)
     update_part = jnp.dot(proj_low, features, preferred_element_type=jnp.float32)
-    update = lax.psum(update_part, "samp")
+    update = jnp.sum(lax.all_gather(update_part, "samp"), axis=0)
     grown = basis + update / math.sqrt(span_total)
     basis_out = cholesky_step(grown, features_total)
     return (basis_out, projections)

time: 160 us -> 144 us (0.900)
  waiting for transfers between devices: 70.7 us -> 54.8 us
  matrix products: 40.6 us -> 38.6 us
    psum x1 -> x0, waiting for transfers between devices: 32.5 us -> none  [local(): update = lax.psum(update_part, 'samp')]
    all_gather x0 -> x1, waiting for transfers between devices: none -> 16.6 us  [local(): update = jnp.sum(lax.all_gather(update_part, 'samp'), axis=0)]
where the time goes in v1:
time: 144 us; the launch traced here: 143 us
  waiting for transfers between devices  54.8 us (38%)
  matrix products  38.6 us (27%)
  blocking collectives  19 us (13%)
  other arithmetic  16.6 us (12%)
  between operations  14.2 us (10%)
    psum x1, waiting for transfers between devices, local(): summed = lax.psum(partial_scores, 'feat')  38.1 us
    dot_general x1, matrix products, local(): jnp.dot(mixed, table, preferred_element_type=jnp.float32) * scale / width  22.2 us
    psum x1, blocking collectives, cholesky_step(): gram = lax.psum(local_gram, 'feat')  19 us
    all_gather x1, waiting for transfers between devices, local(): update = jnp.sum(lax.all_gather(update_part, 'samp'), axis=0)  16.6 us
    dot_general x1, matrix products, local(): picked = jnp.dot(first, reorder, preferred_element_type=jnp.float32)  12.2 us
    another operation x3, other arithmetic, cholesky_step(): lower = jnp.linalg.cholesky(gram / total)  6.52 us
    another operation x2, other arithmetic, cholesky_step(): return jax.scipy.linalg.solve_triangular(lower, grown, lower=True)  5.55 us
  transfers between devices with their start and end apart: 2, of which 2 were waited for; matrix products, arithmetic and copies ran while one was open for 0% of the time, Pallas kernels for 0%

profile of v1, /device:TPU:0, one launch (start us, length us, event | category | flops | bytes accessed | tf_op | source)
XLA Modules:
  0.0 143.3 jit_solution(6783431924705769275)
XLA Ops:
  7.2 0.0 all-reduce.2.cloned.1.call-start
  7.3 0.7 add_convert_fusion
  8.0 1.5 %iota_compare_fusion.7 = pred[1024,1024]{1,0:T(32,128)(4,1)S(1)} fusion(s32[1024]{0:T(1024)} %bitcast.17), kind=kLoop, calls=%fused_computation.7.clone.clone.2 | loop fusion | flops 1048576 | bytes 1052672 | tf_op jit(solution)/shard_map/dot_general | solution.py:36
  9.5 0.0 copy-start.2
  9.5 0.0 copy-start.3
  9.5 0.0 copy-start.4
  9.5 12.2 %fusion.2 = f32[1024,1024]{1,0:T(8,128)} fusion(bf16[1024,1024]{1,0:T(8,128)(2,1)} %param.7, bf16[1024]{0:T(1024)(128)(2,1)S(1)} %add_convert_fusion, s32[1024]{0:T(1024)S(1)} %get-tuple-element.2, s32[1024]{0:T(1024)S(1)} %get-tuple-element.3, s32[1024]{0:T(1024)S(1)} %get-tuple-element.4, s32[1024]{0:T(1024)S(1)} %get-tuple-element.5, ...), kind=kOutput, calls=%fused_computation.9 | convolution fusion | flops 4331667456 | bytes 7383040 | tf_op jit(solution)/shard_map/dot_general | solution.py:36
  21.7 0.0 copy-done.2
  21.7 0.0 copy-done.3
  21.7 0.0 copy-done.4
  21.7 0.0 copy-start
  21.7 22.2 %multiply_convert_fusion = bf16[1024,1024]{1,0:T(8,128)(2,1)S(1)} fusion(f32[1024,1024]{1,0:T(8,128)} %fusion.2, f32[1024]{0:T(1024)S(1)} %copy-done.2, f32[1024]{0:T(1024)S(1)} %copy-done.3, f32[1024]{0:T(1024)S(1)} %copy-done.4, s32[1024]{0:T(1024)S(1)} %get-tuple-element.2, s32[1024]{0:T(1024)S(1)} %get-tuple-element.3, s32[1024]{0:T(1024)S(1)} %get-tuple-element.4, ...), kind=kOutput, calls=%fused_computation.5 | convolution fusion | flops 2189426688 | bytes 6344704 | tf_op jit(solution)/shard_map/dot_general | solution.py:38
  44.0 0.0 copy-done
  44.0 1.5 %convolution_bitcast_fusion = f32[64,1024]{1,0:T(8,128)} fusion(bf16[1024,1024]{1,0:T(8,128)(2,1)S(1)} %multiply_convert_fusion, f32[64,1024]{1,0:T(8,128)S(1)} %copy-done), kind=kOutput, calls=%fused_computation.15 | convolution fusion | flops 134283264 | bytes 2621440 | tf_op jit(solution)/shard_map/dot_general | solution.py:41
  45.4 0.0 all-reduce.2.cloned.1.call-update
  45.5 0.0 all-gather.3.cloned.1.call-start
  45.5 38.1 %all-reduce.2.cloned.1.call-done = f32[64,1024]{1,0:T(8,128)} async-done(((f32[64,1024]{1,0:T(8,128)}), f32[64,1024]{1,0:T(8,128)}) %all-reduce.2.cloned.1.call-update) | async-done | bytes 262160 | tf_op jit(solution)/shard_map/psum | solution.py:44
  83.6 1.0 broadcast_multiply_fusion
  84.6 0.0 copy-start.1
  84.6 1.2 fusion.14
  85.8 0.0 all-gather.3.cloned.1.call-update
  85.8 16.6 %all-gather.3.cloned.1.call-done = f32[256,1024]{1,0:T(8,128)} async-done(((f32[64,1024]{1,0:T(8,128)}), f32[256,1024]{1,0:T(8,128)}) %all-gather.3.cloned.1.call-update) | async-done | bytes 1048592 | tf_op jit(solution)/shard_map/all_gather | solution.py:48
  102.4 1.3 reduce_sum.9
  103.7 0.4 fusion.18
  104.1 19.0 %psum.15 = f32[64,64]{0,1:T(8,128)S(1)} all-reduce(f32[64,64]{0,1:T(8,128)S(1)} %fusion.18), channel_id=1, replica_groups=mesh['grp'=2,'feat'=4,'samp'=4] {'feat'}, use_global_device_ids=true, to_apply=%region_2.3 | all-reduce | flops 4096 | bytes 32768 | tf_op jit(solution)/shard_map/psum | solution.py:20
  123.1 0.1 copy.10
  123.2 5.8 %cholesky.16 = f32[64,64]{1,0:T(8,128)S(1)} custom-call(f32[64,64]{1,0:T(8,128)S(1)} %fusion.21), custom_call_target="Cholesky" | custom-call | tf_op jit(solution)/shard_map/jit(cholesky)/cholesky | solution.py:21
  129.1 0.6 compare_reduce_fusion
  129.7 0.7 fusion.19
  130.4 4.9 %custom-call.7 = f32[1,64,64]{1,2,0:T(8,128)S(1)} custom-call(f32[1,64,64]{2,1,0:T(8,128)S(1)} %fusion.19), custom_call_target="InvertDiagBlocksLowerTriangular" | custom-call | tf_op jit(solution)/shard_map/jit(_solve_triangular)/triangular_solve | solution.py:22
  135.3 1.1 fusion.17
  136.4 0.0 copy-done.1
  (8 shorter events, 0.1 us)
Async XLA Ops:
  7.2 76.5 %all-reduce.2.cloned.1.call-start = ((), (), s32[]{:S(2)}) async-start(), calls=%async_computation | async-start | bytes 524288 | tf_op jit(solution)/shard_map/psum | solution.py:44
  9.5 12.3 %copy-start.2 = (f32[1024]{0:T(1024)S(1)}, f32[1024]{0:T(1024)}, u32[]{:S(2)}) copy-start(f32[1024]{0:T(1024)} %param.12) | copy-start | bytes 12292
  9.5 12.3 %copy-start.3 = (f32[1024]{0:T(1024)S(1)}, f32[1024]{0:T(1024)}, u32[]{:S(2)}) copy-start(f32[1024]{0:T(1024)} %param.11) | copy-start | bytes 12292
  9.5 12.3 %copy-start.4 = (f32[1024]{0:T(1024)S(1)}, f32[1024]{0:T(1024)}, u32[]{:S(2)}) copy-start(f32[1024]{0:T(1024)} %param.10) | copy-start | bytes 12292
  21.7 22.2 %copy-start = (f32[64,1024]{1,0:T(8,128)S(1)}, f32[64,1024]{1,0:T(8,128)}, u32[]{:S(2)}) copy-start(f32[64,1024]{1,0:T(8,128)} %param.13) | copy-start | bytes 786436
  45.5 57.0 %all-gather.3.cloned.1.call-start = ((), (), s32[]{:S(2)}) async-start(), calls=%async_computation.1 | async-start | bytes 1310720 | tf_op jit(solution)/shard_map/all_gather | solution.py:48
  84.6 51.8 %copy-start.1 = (f32[64,1024]{1,0:T(8,128)}, f32[64,1024]{1,0:T(8,128)S(1)}, u32[]{:S(2)}) copy-start(f32[64,1024]{1,0:T(8,128)S(1)} %broadcast_multiply_fusion) | copy-start | bytes 786436
Sparse Core Ops, SparseCore 0:
  45.6 37.9 all-reduce.1
  85.9 16.4 all-gather.2
